TPU v7x, 32 devices: a whole 2x2x4 slice. The times are simulated.
32 devices in a mesh: beam: 2 (over x), freq: 16 (over z, y, core).
Axes of the slice: x: 2, y: 2, z: 4, core: 2. Of those that a mesh axis runs over, the one named last changes fastest.
Arguments:
- spectrum: bfloat16 [2, 65536], P(None, ('beam', 'freq')), parts along dimension 1, may hold values from -6 to 6
- template_bank: bfloat16 [2, 256, 1024], replicated, may hold values from -0.125 to 0.125
- template_index: int32 [128], replicated, may hold values from 0 to 255
Outputs:
- harmonic_sum: float32 [128, 65536], P(None, ('beam', 'freq')), parts along dimension 1
There are 2 independent parts, one for each index of `beam`. A program takes and returns all parts, laid end to end along the dimension named above; an argument that names none is the same for every part. Nothing has to cross between parts.
Inputs may be any that keep to these rules, and one draw needn't show every extreme that they name: `template_index`: entry z names the bank template of acceleration row z.
All inputs are finite; a program needn't handle non-finite values.
Results may differ from a plain program's by a relative error of at most 0.002.
Values may be sent and summed in bfloat16 or wider, within the bound.
A program may use at most 64 MiB of HBM per device.

v0:
```python
import math

import jax
import jax.numpy as jnp
from jax import lax
from jax.sharding import PartitionSpec as P


def with_halo(cells, sides, width):
    for axis, dim in sides:
        count = lax.axis_size(axis)
        ends = count - 1
        head = lax.slice_in_dim(cells, 0, width, axis=dim)
        tail = lax.slice_in_dim(cells, cells.shape[dim] - width, cells.shape[dim], axis=dim)
        cells = jnp.concatenate(
            [
                lax.ppermute(tail, axis, [(i, (i + 1) % count) for i in range(ends)]),
                cells,
                lax.ppermute(head, axis, [((i + 1) % count, i) for i in range(ends)]),
            ],
            axis=dim,
        )
    return cells


def as_sent(array):

    def short(part):
        return part.astype(jnp.bfloat16) if part.dtype == jnp.float32 else part

    return jax.tree.map(short, array)


def correlate(window, template_re, template_im):
    row_count = template_re.shape[0]
    taps = template_re.shape[1]
    length = window.shape[1] - taps
    block = math.gcd(length, 512)
    block_count = length // block
    kernel = jnp.concatenate(
        [jnp.stack([template_re, -template_im], 1), jnp.stack([template_im, template_re], 1)], 0
    )

    def one_block(start):
        segment = lax.dynamic_slice_in_dim(window, start, block + taps, 1)
        correlated = lax.conv_general_dilated(
            segment[None],
            kernel,
            (1,),
            "VALID",
            dimension_numbers=("NCH", "OIH", "NCH"),
            preferred_element_type=jnp.float32,
        )[0]
        real_part = correlated[:row_count, :block]
        imag_part = correlated[row_count:, :block]
        return (real_part * real_part + imag_part * imag_part).astype(jnp.bfloat16)

    starts = jnp.arange(block_count, dtype=jnp.int32) * block
    powers = lax.map(one_block, starts)
    return jnp.transpose(powers, (1, 0, 2)).reshape(row_count, length)


def stretch(source, numerator, denominator):
    row_count, col_count = source.shape
    small_expand = (
        jnp.arange(denominator)[None, :] * numerator // denominator
        == jnp.arange(numerator)[:, None]
    ).astype(jnp.bfloat16)
    grouped = source.reshape(row_count // numerator, numerator, col_count)
    spread = jnp.einsum(
        "anc,nk->akc", grouped, small_expand, preferred_element_type=jnp.float32
    ).astype(jnp.bfloat16)
    new_rows = row_count // numerator * denominator
    group_cols = math.gcd(col_count // numerator, 128)
    block_expand = (
        jnp.arange(denominator * group_cols)[None, :] * numerator // denominator
        == jnp.arange(numerator * group_cols)[:, None]
    ).astype(jnp.bfloat16)
    blocks = spread.reshape(new_rows, col_count // (numerator * group_cols), numerator * group_cols)
    result = jnp.einsum("abn,nk->abk", blocks, block_expand, preferred_element_type=jnp.float32)
    return result.reshape(new_rows, col_count // numerator * denominator)


def tiles_out(columns_held, row_count, numerator, denominator, owners, device, tract_cols):
    span = owners * numerator // denominator
    targets = jnp.arange(owners, dtype=jnp.int32)
    offset = (device - targets * span) % owners
    valid = offset < span
    source_block = jnp.minimum((targets * span + offset) // owners, owners - 1)
    held = columns_held[:row_count].reshape(row_count, owners, tract_cols)
    picked = jnp.take(held, source_block, axis=1)
    picked = jnp.where(valid[None, :, None], picked, jnp.zeros_like(picked))
    return picked.reshape(row_count, owners * tract_cols)


def tiles_in(received, numerator, denominator, owners, device, tract_cols):
    row_count = received.shape[0]
    span = owners * numerator // denominator
    source_owner = (device * span + jnp.arange(span, dtype=jnp.int32)) % owners
    got = jnp.take(received.reshape(row_count, owners, tract_cols), source_owner, axis=1)
    return got.reshape(row_count, span * tract_cols)


def body(spectrum, template_bank, template_index):
    owners = lax.axis_size("freq")
    device = lax.axis_index("freq")
    taps = template_bank.shape[2]
    rows_all = template_index.shape[0]
    half_taps = taps // 2
    tract_cols = spectrum.shape[1] // owners
    one_hot = (
        template_index[:, None] == jnp.arange(template_bank.shape[1], dtype=jnp.int32)[None, :]
    ).astype(jnp.bfloat16)
    template_re = jnp.dot(one_hot, template_bank[0], preferred_element_type=jnp.float32).astype(
        jnp.bfloat16
    )
    template_im = jnp.dot(one_hot, template_bank[1], preferred_element_type=jnp.float32).astype(
        jnp.bfloat16
    )
    padded = with_halo(spectrum, (("freq", 1),), half_taps)
    plane = correlate(padded, template_re, template_im)
    held_rows = 3 * rows_all // 4
    columns_held = lax.all_to_all(
        as_sent(plane[:held_rows]), "freq", split_axis=1, concat_axis=1, tiled=True
    )
    total = plane.astype(jnp.float32)
    half_send = tiles_out(columns_held, rows_all // 2, 1, 2, owners, device, tract_cols)
    half_got = lax.all_to_all(
        as_sent(half_send), "freq", split_axis=1, concat_axis=1, tiled=True
    ).astype(half_send.dtype)
    total = total + stretch(tiles_in(half_got, 1, 2, owners, device, tract_cols), 1, 2)
    quarter_send = tiles_out(columns_held, rows_all // 4, 1, 4, owners, device, tract_cols)
    quarter_got = lax.all_to_all(
        as_sent(quarter_send), "freq", split_axis=1, concat_axis=1, tiled=True
    ).astype(quarter_send.dtype)
    total = total + stretch(tiles_in(quarter_got, 1, 4, owners, device, tract_cols), 1, 4)
    three_send = tiles_out(columns_held, held_rows, 3, 4, owners, device, tract_cols)
    three_got = lax.all_to_all(
        as_sent(three_send), "freq", split_axis=1, concat_axis=1, tiled=True
    ).astype(three_send.dtype)
    total = total + stretch(tiles_in(three_got, 3, 4, owners, device, tract_cols), 3, 4)
    return total


def solution(mesh):
    return jax.shard_map(
        body,
        mesh=mesh,
        in_specs=(P(None, ("beam", "freq")), P(), P()),
        out_specs=P(None, ("beam", "freq")),
        check_vma=False,
    )
```

profile of v0, /device:TPU:1, one launch (start us, length us, event | category | flops | bytes accessed | tf_op | source)
XLA Modules:
  0.0 281.0 jit_solution(6663480286862663322)
XLA Ops:
  0.0 0.7 fusion.67
  0.7 4.5 %collective-permute-start = (bf16[2,512]{1,0:T(2,128)(2,1)S(1)}, bf16[2,512]{1,0:T(2,128)(2,1)S(1)}, u32[]{:S(2)}, u32[]{:S(2)}) collective-permute-start(bf16[2,512]{1,0:T(2,128)(2,1)S(1)} %get-tuple-element.68), channel_id=1, source_target_pairs={{0,1},{1,2},{2,3},{3,4},{4,5},{5,6},{6,7},{7,8},{8,9},{9,10},{10,1... | collective-permute-start | bytes 6152 | tf_op jit(solution)/shard_map/ppermute | solution.py:17
  5.2 1.9 collective-permute-start.1
  7.2 0.5 fusion.61
  7.7 0.5 compare_and_fusion.5
  8.2 0.5 fusion.63
  8.7 0.6 compare_and_fusion.3
  9.3 0.5 fusion.65
  9.8 0.6 compare_and_fusion.1
  10.4 0.6 fusion.62
  11.1 0.6 and_select_fusion.14
  11.6 0.6 compare_and_fusion.2
  12.2 0.6 compare_and_fusion
  12.8 0.6 compare_and_fusion.4
  13.4 0.6 add_select_fusion.1
  14.0 0.6 add_select_fusion
  14.6 1.3 convolution_convert_fusion.1
  15.9 1.3 fusion.5
  17.3 0.6 pad_clamp_fusion.5
  17.9 0.6 pad_clamp_fusion.1
  18.6 0.6 fusion.47
  19.2 0.9 copy.47
  20.2 195.0 %while.10 = (s32[]{:T(128)}, bf16[4,128,512]{1,2,0:T(8,128)(2,1)S(1)}, s32[4]{0:T(128)S(1)}, bf16[2,3072]{1,0:T(2,128)(2,1)S(1)}, bf16[256,2,1024]{0,1,2:T(2,128)(2,1)S(1)}, /*index=5*/s32[]{:T(128)}, s32[]{:T(128)}, s32[]{:T(128)}) while((s32[]{:T(128)}, bf16[4,128,512]{1,2,0:T(8,128)(2,1)S(1)}, s32[4]{0:T(128)S(1)}, ...), condition=%wide.region_1.2_spmd, body=%wide.region_0.1_spmd.sunk | while | flops 538181632 | bytes 3310739 | solution.py:59
  20.4 0.6 dynamic_slice.11
  23.0 0.6 copy.80
  23.7 38.6 %fusion.77 = f32[1,256,513]{1,0,2:T(1,128)S(1)} fusion(bf16[1,2,1536]{1,0,2:T(2,128)(2,1)S(1)} %copy.80, bf16[256,2,1024]{0,1,2:T(2,128)(2,1)S(1)} %get-tuple-element.127), kind=kOutput, calls=%fused_computation.215.clone.1 | convolution fusion | flops 537919488 | bytes 1580032 | tf_op jit(solution)/shard_map/while/body/eval_jaxpr/conv_general_dilated | solution.py:46
  68.4 0.6 dynamic_slice.11
  71.0 0.6 copy.80
  71.7 38.5 %fusion.77 = f32[1,256,513]{1,0,2:T(1,128)S(1)} fusion(bf16[1,2,1536]{1,0,2:T(2,128)(2,1)S(1)} %copy.80, bf16[256,2,1024]{0,1,2:T(2,128)(2,1)S(1)} %get-tuple-element.127), kind=kOutput, calls=%fused_computation.215.clone.1 | convolution fusion | flops 537919488 | bytes 1580032 | tf_op jit(solution)/shard_map/while/body/eval_jaxpr/conv_general_dilated | solution.py:46
  116.0 0.6 dynamic_slice.11
  118.6 0.6 copy.80
  119.2 38.5 %fusion.77 = f32[1,256,513]{1,0,2:T(1,128)S(1)} fusion(bf16[1,2,1536]{1,0,2:T(2,128)(2,1)S(1)} %copy.80, bf16[256,2,1024]{0,1,2:T(2,128)(2,1)S(1)} %get-tuple-element.127), kind=kOutput, calls=%fused_computation.215.clone.1 | convolution fusion | flops 537919488 | bytes 1580032 | tf_op jit(solution)/shard_map/while/body/eval_jaxpr/conv_general_dilated | solution.py:46
  163.8 0.6 dynamic_slice.11
  166.4 0.6 copy.80
  167.0 38.5 %fusion.77 = f32[1,256,513]{1,0,2:T(1,128)S(1)} fusion(bf16[1,2,1536]{1,0,2:T(2,128)(2,1)S(1)} %copy.80, bf16[256,2,1024]{0,1,2:T(2,128)(2,1)S(1)} %get-tuple-element.127), kind=kOutput, calls=%fused_computation.215.clone.1 | convolution fusion | flops 537919488 | bytes 1580032 | tf_op jit(solution)/shard_map/while/body/eval_jaxpr/conv_general_dilated | solution.py:46
  215.3 0.9 copy.49
  216.2 6.5 %all-to-all-start = ((bf16[96,16,128]{2,0,1:T(8,128)(2,1)}), bf16[96,16,128]{2,0,1:T(8,128)(2,1)S(1)}, u32[]{:S(2)}, u32[]{:S(2)}) async-start(bf16[96,16,128]{2,0,1:T(8,128)(2,1)} %copy.49), calls=%async_computation | async-start | bytes 786432 | tf_op jit(solution)/shard_map/all_to_all | solution.py:123
  222.9 11.7 %all-to-all-done = bf16[96,16,128]{2,0,1:T(8,128)(2,1)S(1)} async-done(((bf16[96,16,128]{2,0,1:T(8,128)(2,1)}), bf16[96,16,128]{2,0,1:T(8,128)(2,1)S(1)}, u32[]{:S(2)}, u32[]{:S(2)}) %all-to-all-start) | async-done | bytes 393248 | tf_op jit(solution)/shard_map/all_to_all | solution.py:123
  234.5 0.6 gather_fusion.2
  235.2 0.8 select_bitcast_fusion.2
  235.9 3.9 %all-to-all-start.2 = ((bf16[32,16,128]{2,0,1:T(8,128)(2,1)}), bf16[32,16,128]{2,0,1:T(8,128)(2,1)S(1)}, u32[]{:S(2)}, u32[]{:S(2)}) async-start(bf16[32,16,128]{2,0,1:T(8,128)(2,1)} %select_bitcast_fusion.2), calls=%async_computation.2 | async-start | bytes 262144 | tf_op jit(solution)/shard_map/all_to_all | solution.py:133
  239.8 0.7 gather_fusion
  240.6 0.7 gather_fusion.4
  241.3 0.8 select_bitcast_fusion.1
  242.2 4.5 %all-to-all-done.2 = bf16[32,16,128]{2,0,1:T(8,128)(2,1)S(1)} async-done(((bf16[32,16,128]{2,0,1:T(8,128)(2,1)}), bf16[32,16,128]{2,0,1:T(8,128)(2,1)S(1)}, u32[]{:S(2)}, u32[]{:S(2)}) %all-to-all-start.2) | async-done | bytes 131104 | tf_op jit(solution)/shard_map/all_to_all | solution.py:133
  246.6 4.5 %all-to-all-start.1 = ((bf16[64,16,128]{2,0,1:T(8,128)(2,1)}), bf16[64,16,128]{2,0,1:T(8,128)(2,1)S(1)}, u32[]{:S(2)}, u32[]{:S(2)}) async-start(bf16[64,16,128]{2,0,1:T(8,128)(2,1)} %select_bitcast_fusion.1), calls=%async_computation.1 | async-start | bytes 524288 | tf_op jit(solution)/shard_map/all_to_all | solution.py:128
  251.2 0.9 select_bitcast_fusion
  252.0 0.6 gather_fusion.3
  252.9 7.9 %all-to-all-done.1 = bf16[64,16,128]{2,0,1:T(8,128)(2,1)S(1)} async-done(((bf16[64,16,128]{2,0,1:T(8,128)(2,1)}), bf16[64,16,128]{2,0,1:T(8,128)(2,1)S(1)}, u32[]{:S(2)}, u32[]{:S(2)}) %all-to-all-start.1) | async-done | bytes 262176 | tf_op jit(solution)/shard_map/all_to_all | solution.py:128
  260.7 4.0 %all-to-all-start.3 = ((bf16[96,16,128]{2,0,1:T(8,128)(2,1)}), bf16[96,16,128]{2,0,1:T(8,128)(2,1)S(1)}, u32[]{:S(2)}, u32[]{:S(2)}) async-start(bf16[96,16,128]{2,0,1:T(8,128)(2,1)} %select_bitcast_fusion), calls=%async_computation.3 | async-start | bytes 786432 | tf_op jit(solution)/shard_map/all_to_all | solution.py:138
  264.7 0.3 fusion.23
  265.1 0.6 gather_fusion.1
  265.7 0.2 fusion.19
  266.0 0.2 reshape.1005
  266.2 0.3 fusion.20
  266.5 10.1 %all-to-all-done.3 = bf16[96,16,128]{2,0,1:T(8,128)(2,1)S(1)} async-done(((bf16[96,16,128]{2,0,1:T(8,128)(2,1)}), bf16[96,16,128]{2,0,1:T(8,128)(2,1)S(1)}, u32[]{:S(2)}, u32[]{:S(2)}) %all-to-all-start.3) | async-done | bytes 393248 | tf_op jit(solution)/shard_map/all_to_all | solution.py:138
  276.6 0.6 gather_fusion.5
  277.4 0.1 gather.32
  277.5 0.4 fusion.4
  278.0 0.1 reshape.1011
  278.2 0.5 fusion.9
  278.7 0.5 copy-done.1
  279.3 0.2 fusion.7
  279.5 1.3 copy.59
  (74 shorter events, 1.7 us)
Async XLA Ops:
  0.7 19.4 %collective-permute-start = (bf16[2,512]{1,0:T(2,128)(2,1)S(1)}, bf16[2,512]{1,0:T(2,128)(2,1)S(1)}, u32[]{:S(2)}, u32[]{:S(2)}) collective-permute-start(bf16[2,512]{1,0:T(2,128)(2,1)S(1)} %get-tuple-element.68), channel_id=1, source_target_pairs={{0,1},{1,2},{2,3},{3,4},{4,5},{5,6},{6,7},{7,8},{8,9},{9,10},{10,1... | collective-permute-start | bytes 6152 | tf_op jit(solution)/shard_map/ppermute | solution.py:17
  5.2 14.9 %collective-permute-start.1 = (bf16[2,512]{1,0:T(2,128)(2,1)S(1)}, bf16[2,512]{1,0:T(2,128)(2,1)S(1)}, u32[]{:S(2)}, u32[]{:S(2)}) collective-permute-start(bf16[2,512]{1,0:T(2,128)(2,1)S(1)} %get-tuple-element.69), channel_id=1, source_target_pairs={{1,0},{2,1},{3,2},{4,3},{5,4},{6,5},{7,6},{8,7},{9,8},{10,9},{11,1... | collective-permute-start | bytes 6152 | tf_op jit(solution)/shard_map/ppermute | solution.py:19
  19.2 1.0 copy-start.2
  215.2 19.9 %copy-start = (bf16[4,128,512]{1,2,0:T(8,128)(2,1)}, bf16[4,128,512]{1,2,0:T(8,128)(2,1)S(1)}, u32[]{:S(2)}) copy-start(bf16[4,128,512]{1,2,0:T(8,128)(2,1)S(1)} %get-tuple-element.32) | copy-start | bytes 1572868
  215.2 7.5 %copy-start.17 = (s32[16]{0:T(128)S(1)}, s32[16]{0:T(128)}, u32[]{:S(2)}) copy-start(s32[16]{0:T(128)} %fusion.62) | copy-start | bytes 196
  215.2 7.5 %copy-start.16 = (s32[12]{0:T(128)S(1)}, s32[12]{0:T(128)}, u32[]{:S(2)}) copy-start(s32[12]{0:T(128)} %fusion.65) | copy-start | bytes 148
  215.2 7.5 %copy-start.14 = (s32[4]{0:T(128)S(1)}, s32[4]{0:T(128)}, u32[]{:S(2)}) copy-start(s32[4]{0:T(128)} %fusion.63) | copy-start | bytes 52
  215.2 7.5 %copy-start.13 = (s32[8]{0:T(128)S(1)}, s32[8]{0:T(128)}, u32[]{:S(2)}) copy-start(s32[8]{0:T(128)} %fusion.61) | copy-start | bytes 100
  215.2 7.5 %copy-start.15 = (pred[12]{0:T(512)(128)(4,1)S(1)}, pred[12]{0:T(512)(128)(4,1)}, u32[]{:S(2)}) copy-start(pred[12]{0:T(512)(128)(4,1)} %compare_and_fusion.1) | copy-start | bytes 40
  215.2 19.9 %copy-start.11 = (pred[16]{0:T(512)(128)(4,1)S(1)}, pred[16]{0:T(512)(128)(4,1)}, u32[]{:S(2)}) copy-start(pred[16]{0:T(512)(128)(4,1)} %get-tuple-element.72) | copy-start | bytes 52
  215.3 19.9 %copy-start.12 = (pred[16]{0:T(512)(128)(4,1)S(1)}, pred[16]{0:T(512)(128)(4,1)}, u32[]{:S(2)}) copy-start(pred[16]{0:T(512)(128)(4,1)} %get-tuple-element.73) | copy-start | bytes 52
  216.2 18.3 %all-to-all-start = ((bf16[96,16,128]{2,0,1:T(8,128)(2,1)}), bf16[96,16,128]{2,0,1:T(8,128)(2,1)S(1)}, u32[]{:S(2)}, u32[]{:S(2)}) async-start(bf16[96,16,128]{2,0,1:T(8,128)(2,1)} %copy.49), calls=%async_computation | async-start | bytes 786432 | tf_op jit(solution)/shard_map/all_to_all | solution.py:123
  235.9 5.4 %copy-start.18 = (pred[16]{0:T(512)(128)(4,1)S(1)}, pred[16]{0:T(512)(128)(4,1)}, u32[]{:S(2)}) copy-start(pred[16]{0:T(512)(128)(4,1)} %get-tuple-element.74) | copy-start | bytes 52
  235.9 5.4 %copy-start.19 = (pred[16]{0:T(512)(128)(4,1)S(1)}, pred[16]{0:T(512)(128)(4,1)}, u32[]{:S(2)}) copy-start(pred[16]{0:T(512)(128)(4,1)} %get-tuple-element.75) | copy-start | bytes 52
  235.9 10.7 %all-to-all-start.2 = ((bf16[32,16,128]{2,0,1:T(8,128)(2,1)}), bf16[32,16,128]{2,0,1:T(8,128)(2,1)S(1)}, u32[]{:S(2)}, u32[]{:S(2)}) async-start(bf16[32,16,128]{2,0,1:T(8,128)(2,1)} %select_bitcast_fusion.2), calls=%async_computation.2 | async-start | bytes 262144 | tf_op jit(solution)/shard_map/all_to_all | solution.py:133
  240.5 10.6 %copy-start.8 = (pred[16]{0:T(512)(128)(4,1)S(1)}, pred[16]{0:T(512)(128)(4,1)}, u32[]{:S(2)}) copy-start(pred[16]{0:T(512)(128)(4,1)} %get-tuple-element.70) | copy-start | bytes 52
  240.5 10.6 %copy-start.9 = (pred[16]{0:T(512)(128)(4,1)S(1)}, pred[16]{0:T(512)(128)(4,1)}, u32[]{:S(2)}) copy-start(pred[16]{0:T(512)(128)(4,1)} %get-tuple-element.71) | copy-start | bytes 52
  241.3 11.3 %copy-start.7 = (pred[4]{0:T(512)(128)(4,1)S(1)}, pred[4]{0:T(512)(128)(4,1)}, u32[]{:S(2)}) copy-start(pred[4]{0:T(512)(128)(4,1)} %compare_and_fusion.3) | copy-start | bytes 16
  241.3 11.4 %copy-start.10 = (f32[4]{0:T(128)S(1)}, f32[4]{0:T(128)}, u32[]{:S(2)}) copy-start(f32[4]{0:T(128)} %fusion.47) | copy-start | bytes 52
  246.6 14.1 %all-to-all-start.1 = ((bf16[64,16,128]{2,0,1:T(8,128)(2,1)}), bf16[64,16,128]{2,0,1:T(8,128)(2,1)S(1)}, u32[]{:S(2)}, u32[]{:S(2)}) async-start(bf16[64,16,128]{2,0,1:T(8,128)(2,1)} %select_bitcast_fusion.1), calls=%async_computation.1 | async-start | bytes 524288 | tf_op jit(solution)/shard_map/all_to_all | solution.py:128
  251.2 13.5 %copy-start.4 = (s32[512]{0:T(512)S(1)}, s32[512]{0:T(512)}, u32[]{:S(2)}) copy-start(s32[512]{0:T(512)} %add_select_fusion.1) | copy-start | bytes 6148
  252.9 12.8 %copy-start.6 = (pred[8]{0:T(512)(128)(4,1)S(1)}, pred[8]{0:T(512)(128)(4,1)}, u32[]{:S(2)}) copy-start(pred[8]{0:T(512)(128)(4,1)} %compare_and_fusion.5) | copy-start | bytes 28
  260.7 15.9 %all-to-all-start.3 = ((bf16[96,16,128]{2,0,1:T(8,128)(2,1)}), bf16[96,16,128]{2,0,1:T(8,128)(2,1)S(1)}, u32[]{:S(2)}, u32[]{:S(2)}) async-start(bf16[96,16,128]{2,0,1:T(8,128)(2,1)} %select_bitcast_fusion), calls=%async_computation.3 | async-start | bytes 786432 | tf_op jit(solution)/shard_map/all_to_all | solution.py:138
  265.0 1.1 copy-start.5
  277.5 0.7 copy-start.3
  278.2 1.0 copy-start.1
where the time goes:
time: 284 us; the launch traced here: 281 us
  matrix products  158 us (56%)
  loops' own time  35 us (12%)
  waiting for transfers between devices  34.1 us (12%)
  starting transfers between devices  25.2 us (9%)
  local copies, waits for them, and re-layouts  14.8 us (5%)
  other arithmetic  12.8 us (5%)
    conv_general_dilated x4, matrix products, one_block(): lax.conv_general_dilated(segment[None], kernel, (1,), 'VALID', dimension_...  154 us
    another operation x1, loops' own time, correlate(): powers = lax.map(one_block, starts)  35 us
    all_to_all x1, waiting for transfers between devices, body(): lax.all_to_all(as_sent(plane[:held_rows]), 'freq', split_axis=1, concat_a...  11.7 us
    all_to_all x1, waiting for transfers between devices, body(): lax.all_to_all(as_sent(three_send), 'freq', split_axis=1, concat_axis=1,...  10.1 us
    all_to_all x1, waiting for transfers between devices, body(): lax.all_to_all(as_sent(half_send), 'freq', split_axis=1, concat_axis=1, t...  7.85 us
    all_to_all x1, starting transfers between devices, body(): lax.all_to_all(as_sent(plane[:held_rows]), 'freq', split_axis=1, concat_a...  6.45 us
  transfers between devices with their start and end apart: 6, of which 4 were waited for; matrix products, arithmetic and copies ran while one was open for 7% of the time, Pallas kernels for 0%

commit v1 on v0

v1 whole, which is shorter than its diff:
```python
import functools

import jax
import jax.numpy as jnp
from jax import lax
from jax.experimental import pallas as pl
from jax.experimental.pallas import tpu as pltpu
from jax.sharding import PartitionSpec as P

RATIOS = ((1, 1), (1, 2), (1, 4), (3, 4))
CHUNK = 256
LANES = 128


class Plan:
    def __init__(self, cols, taps, rows, owners):
        self.cols, self.taps, self.rows, self.owners = cols, taps, rows, owners
        self.granule = taps // 2
        self.held = cols // self.granule
        self.steps = [self.held * n // d for n, d in RATIOS]
        self.part_cols = [cols * n // d for n, d in RATIOS]
        self.part_rows = [rows * n // d for n, d in RATIOS]
        self.offsets, self.slots = [], []
        offset = slot = 0
        for width in self.part_cols:
            self.offsets.append(offset)
            self.slots.append(slot)
            offset += width + taps
            slot += (width + taps) // self.granule
        self.width, self.slot_count = offset, slot


def sends(plan, me):
    found = []
    for own in range(plan.held):
        for part, step in enumerate(plan.steps):
            spot = plan.held * me + own + 1
            last = spot // step
            rest = spot - last * step
            for back in range((step + 1) // step + 1):
                if plan.held % step == 0:
                    if (own + 1) % step + step * back >= step + 2:
                        continue
                to = last - back
                place = rest + step * back
                fits = (to >= 0) & (to < plan.owners) & (place < step + 2)
                found.append((own, part, to, place, fits))
    return found


def gather_kernel(plan, spec_ref, index_ref, bank_ref, win_ref, lhs_ref, bank, bank_sem, send_sems, recv_sems):
    me = lax.axis_index("freq")
    size = plan.granule
    rows = plan.rows
    fetch = pltpu.make_async_copy(bank_ref, bank, bank_sem)
    fetch.start()
    barrier = pltpu.get_barrier_semaphore()

    def greet(step, carry):
        peer = lax.rem(me + step, plan.owners)
        pl.semaphore_signal(barrier, inc=1, device_id={"freq": peer}, device_id_type=pl.DeviceIdType.MESH)
        return carry

    lax.fori_loop(1, plan.owners, greet, 0)

    @pl.when(me == 0)
    def _():
        for offset in plan.offsets:
            win_ref[:, offset : offset + size] = jnp.zeros((2, size), win_ref.dtype)

    @pl.when(me == plan.owners - 1)
    def _():
        end = plan.offsets[0] + plan.part_cols[0] + plan.taps
        win_ref[:, end - size : end] = jnp.zeros((2, size), win_ref.dtype)

    pl.semaphore_wait(barrier, plan.owners - 1)

    def each(act_remote, act_local):
        for number, (own, part, to, place, fits) in enumerate(sends(plan, me)):
            source = spec_ref.at[:, own * size : (own + 1) * size]
            target = win_ref.at[:, pl.ds(pl.multiple_of(plan.offsets[part] + place * size, size), size)]
            got = recv_sems.at[plan.slots[part] + place]

            @pl.when(fits & (to != me))
            def _():
                act_remote(
                    pltpu.make_async_remote_copy(
                        src_ref=source,
                        dst_ref=target,
                        send_sem=send_sems.at[number],
                        recv_sem=got,
                        device_id={"freq": to},
                        device_id_type=pl.DeviceIdType.MESH,
                    )
                )

            if act_local is not None:

                @pl.when(fits & (to == me))
                def _():
                    act_local(pltpu.make_async_copy(source, target, got))

    each(lambda copy: copy.start(), lambda copy: copy.start())

    fetch.wait()
    names = lax.broadcasted_iota(jnp.int32, (bank.shape[1], rows), 0)
    picks = (names == index_ref[...]).astype(jnp.float32).T.astype(jnp.bfloat16)
    real = jnp.dot(picks, bank[0], preferred_element_type=jnp.float32).astype(jnp.bfloat16)
    imag = jnp.dot(picks, bank[1], preferred_element_type=jnp.float32).astype(jnp.bfloat16)
    lhs_ref[0, :rows] = real
    lhs_ref[0, rows:] = imag
    lhs_ref[1, :rows] = -imag
    lhs_ref[1, rows:] = real

    for part, step in enumerate(plan.steps):
        for place in range(step + 2):
            spot = step * me - 1 + place

            @pl.when((spot >= 0) & (spot < plan.held * plan.owners))
            def _():
                start = plan.offsets[part] + place * size
                pltpu.make_async_copy(
                    spec_ref.at[:, 0:size],
                    win_ref.at[:, start : start + size],
                    recv_sems.at[plan.slots[part] + place],
                ).wait()

    each(lambda copy: copy.wait_send(), None)


def one_hot(shape, make):
    left = lax.broadcasted_iota(jnp.int32, shape, 0)
    right = lax.broadcasted_iota(jnp.int32, shape, 1)
    return make(left, right).astype(jnp.float32).astype(jnp.bfloat16)


def search_kernel(plan, win_ref, lhs_ref, out_ref, shifts_re, shifts_im, half_ref, quarter_ref, three_ref):
    rows, taps = plan.rows, plan.taps
    width = plan.width
    blocks = width // LANES

    for which, shifts in ((0, shifts_re), (1, shifts_im)):
        base = jnp.broadcast_to(win_ref[which : which + 1, :].astype(jnp.float32), (16, width))
        place = lax.broadcasted_iota(jnp.int32, (16, width), 0)
        for bit in (1, 2, 4, 8):
            base = jnp.where((place & bit) != 0, pltpu.roll(base, width - bit, 1), base)
        base = base.astype(jnp.bfloat16)
        for turn in range(LANES // 16):
            moved = base if turn == 0 else pltpu.roll(base, width - 16 * turn, 1)
            for block in range(blocks):
                piece = moved[:, block * LANES : (block + 1) * LANES]
                spot = block * LANES + 16 * turn
                shifts[spot : spot + 16, 0:LANES] = piece
                if block:
                    shifts[spot - LANES : spot - LANES + 16, LANES : 2 * LANES] = piece

    def power(part, chunk):
        count = plan.part_rows[part]
        start = pl.multiple_of(plan.offsets[part] + chunk * CHUNK, CHUNK)

        def left(which):
            if count == rows:
                return lhs_ref[which]
            return jnp.concatenate([lhs_ref[which, :count], lhs_ref[which, rows : rows + count]], 0)

        both = jnp.dot(left(0), shifts_re[pl.ds(start, taps), :], preferred_element_type=jnp.float32)
        both += jnp.dot(left(1), shifts_im[pl.ds(start, taps), :], preferred_element_type=jnp.float32)
        real, imag = both[:count], both[count:]
        return (real * real + imag * imag).astype(jnp.bfloat16)

    for part, held in ((1, half_ref), (2, quarter_ref), (3, three_ref)):
        n, d = RATIOS[part]
        spread = one_hot((rows, plan.part_rows[part]), lambda z, k: z * n // d == k)

        def fill(chunk, carry):
            cells = jnp.dot(spread, power(part, chunk), preferred_element_type=jnp.float32)
            held[:, pl.ds(pl.multiple_of(chunk * CHUNK, CHUNK), CHUNK)] = cells.astype(jnp.bfloat16)
            return carry

        lax.fori_loop(0, plan.part_cols[part] // CHUNK, fill, 0)

    half = one_hot((LANES, CHUNK), lambda k, r: k == r // 2)
    quarters = [one_hot((LANES, CHUNK), lambda k, r: k == CHUNK // 4 * odd + r // 4) for odd in (0, 1)]
    threes = [one_hot((CHUNK, CHUNK), lambda k, r: k == CHUNK // 4 * odd + 3 * r // 4) for odd in (0, 1)]
    spreads = [jnp.concatenate([half, quarters[odd], threes[odd]], 0) for odd in (0, 1)]

    def pair(step, carry):
        for odd in (0, 1):
            chunk = 2 * step + odd
            total = power(0, chunk).astype(jnp.float32)
            cells = jnp.concatenate(
                [
                    half_ref[:, pl.ds(pl.multiple_of(chunk * LANES, LANES), LANES)],
                    quarter_ref[:, pl.ds(pl.multiple_of(step * LANES, LANES), LANES)],
                    three_ref[:, pl.ds(pl.multiple_of(step * 3 * LANES + odd * LANES, LANES), CHUNK)],
                ],
                1,
            )
            total += jnp.dot(cells, spreads[odd], preferred_element_type=jnp.float32)
            out_ref[:, pl.ds(pl.multiple_of(chunk * CHUNK, CHUNK), CHUNK)] = total
        return carry

    lax.fori_loop(0, plan.cols // (2 * CHUNK), pair, 0)


def body(spectrum, template_bank, template_index):
    owners = lax.axis_size("freq")
    bank_count, taps = template_bank.shape[1:]
    rows = template_index.shape[0]
    cols = spectrum.shape[1]
    plan = Plan(cols, taps, rows, owners)
    send_count = len(sends(plan, 0))
    vmem = pl.BlockSpec(memory_space=pltpu.VMEM)
    windows, lhs = pl.pallas_call(
        functools.partial(gather_kernel, plan),
        out_shape=(
            jax.ShapeDtypeStruct((2, plan.width), jnp.bfloat16),
            jax.ShapeDtypeStruct((2, 2 * rows, taps), jnp.bfloat16),
        ),
        in_specs=[pl.BlockSpec(memory_space=pl.ANY), vmem, pl.BlockSpec(memory_space=pl.ANY)],
        out_specs=(vmem, vmem),
        scratch_shapes=[
            pltpu.VMEM(template_bank.shape, jnp.bfloat16),
            pltpu.SemaphoreType.DMA,
            pltpu.SemaphoreType.DMA((send_count,)),
            pltpu.SemaphoreType.DMA((plan.slot_count,)),
        ],
        compiler_params=pltpu.CompilerParams(
            collective_id=0, has_side_effects=True, vmem_limit_bytes=16 << 20
        ),
        name="gather",
    )(spectrum, template_index.reshape(1, rows), template_bank)
    return pl.pallas_call(
        functools.partial(search_kernel, plan),
        out_shape=jax.ShapeDtypeStruct((rows, cols), jnp.float32),
        in_specs=[vmem, vmem],
        out_specs=vmem,
        scratch_shapes=[
            pltpu.VMEM((plan.width, CHUNK), jnp.bfloat16),
            pltpu.VMEM((plan.width, CHUNK), jnp.bfloat16),
            pltpu.VMEM((rows, plan.part_cols[1]), jnp.bfloat16),
            pltpu.VMEM((rows, plan.part_cols[2]), jnp.bfloat16),
            pltpu.VMEM((rows, plan.part_cols[3]), jnp.bfloat16),
        ],
        compiler_params=pltpu.CompilerParams(vmem_limit_bytes=32 << 20),
        name="search",
    )(windows, lhs)


def solution(mesh):
    return jax.shard_map(
        body,
        mesh=mesh,
        in_specs=(P(None, ("beam", "freq")), P(), P()),
        out_specs=P(None, ("beam", "freq")),
        check_vma=False,
    )
```

time: 284 us -> 23.4 us (0.08)
  matrix products: 158 us -> 0 us
  loops' own time: 35 us -> 0 us
  waiting for transfers between devices: 34.1 us -> 0 us
  starting transfers between devices: 25.2 us -> 0 us
  Pallas kernels: 0 us -> 20.6 us
  other arithmetic: 12.8 us -> 0 us
  local copies, waits for them, and re-layouts: 14.8 us -> 2.58 us
    conv_general_dilated x4 -> x0, matrix products: 154 us -> none  [one_block(): lax.conv_general_dilated(segment[None], kernel, (1,), 'VALID', dimension_...]
    another operation x1 -> x0, loops' own time: 35 us -> none  [correlate(): powers = lax.map(one_block, starts)]
    all_to_all x4 -> x0, waiting for transfers between devices: 34.1 us -> none  [the longest x1 11.7 us: body(): lax.all_to_all(as_sent(plane[:held_rows]), 'freq', split_axis=1, concat_a...]
    pallas_call x0 -> x2, Pallas kernels: none -> 20.6 us  [the longest x1 12.4 us: body(): pl.pallas_call(functools.partial(search_kernel, plan), out_shape=jax.Shap...]
    all_to_all x4 -> x0, starting transfers between devices: 18.8 us -> none  [the longest x1 6.45 us: body(): lax.all_to_all(as_sent(plane[:held_rows]), 'freq', split_axis=1, concat_a...]
    ppermute x2 -> x0, starting transfers between devices: 6.43 us -> none  [the longest x1 4.51 us: with_halo(): lax.ppermute(tail, axis, [(i, (i + 1) % count) for i in range(ends)])]
    select_n x13 -> x0, other arithmetic: 6.37 us -> none  [the longest x3 2.42 us: tiles_out(): picked = jnp.where(valid[None, :, None], picked, jnp.zeros_like(picked))]
    dot_general x6 -> x0, matrix products: 4.24 us -> none  [the longest x1 1.32 us: body(): jnp.dot(one_hot, template_bank[0], preferred_element_type=jnp.float32)]
  transfers between devices with their start and end apart: 6 -> 0, of which waited for: 4 -> 0; matrix products, arithmetic and copies ran while one was open for 7% -> 0% of each run, Pallas kernels for 0% -> 0%
where the time goes in v1:
time: 23.4 us; the launch traced here: 23.2 us
  Pallas kernels  20.6 us (88%)
  local copies, waits for them, and re-layouts  2.58 us (11%)
    pallas_call x1, Pallas kernels, body(): pl.pallas_call(functools.partial(search_kernel, plan), out_shape=jax.Shap...  12.4 us
    pallas_call x1, Pallas kernels, body(): pl.pallas_call(functools.partial(gather_kernel, plan), out_shape=(jax.Sha...  8.21 us
    unnamed x6, local copies, waits for them, and re-layouts  2.58 us

profile of v1, /device:TPU:1, one launch (start us, length us, event | category | flops | bytes accessed | tf_op | source)
XLA Modules:
  0.0 23.2 jit_solution(5897996898041818350)
XLA Ops:
  0.0 0.0 copy-start.2
  0.0 0.7 %copy-done.2 = s32[128]{0:T(128)S(1)} copy-done((s32[128]{0:T(128)S(1)}, s32[128]{0:T(128)}, u32[]{:S(2)}) %copy-start.2) | copy-done | bytes 536
  0.7 0.0 copy-start
  0.7 1.2 %copy-done = bf16[2,256,1024]{2,1,0:T(8,128)(2,1)S(1)} copy-done((bf16[2,256,1024]{2,1,0:T(8,128)(2,1)S(1)}, bf16[2,256,1024]{2,1,0:T(8,128)(2,1)}, u32[]{:S(2)}) %copy-start) | copy-done | bytes 1048600
  1.9 0.0 copy-start.1
  1.9 0.7 %copy-done.1 = bf16[2,2048]{1,0:T(2,128)(2,1)S(1)} copy-done((bf16[2,2048]{1,0:T(2,128)(2,1)S(1)}, bf16[2,2048]{1,0:T(2,128)(2,1)}, u32[]{:S(2)}) %copy-start.1) | copy-done | bytes 8216
  2.6 8.2 %gather.1 = (bf16[2,9216]{1,0:T(2,128)(2,1)S(1)}, bf16[2,256,1024]{2,1,0:T(8,128)(2,1)S(1)}) custom-call(bf16[2,2048]{1,0:T(2,128)(2,1)S(1)} %copy-done.1, s32[1,128]{1,0:T(1,128)S(1)} %bitcast.1, bf16[2,256,1024]{2,1,0:T(8,128)(2,1)S(1)} %copy-done), custom_call_target="tpu_custom_call" | custom-call | tf_op jit(solution)/shard_map/gather/pallas_call | solution.py:214
  10.8 12.4 %search.1 = f32[128,2048]{1,0:T(8,128)} custom-call(bf16[2,9216]{1,0:T(2,128)(2,1)S(1)} %get-tuple-element.7.win_ref, bf16[2,256,1024]{2,1,0:T(8,128)(2,1)S(1)} %get-tuple-element.8.lhs_ref), custom_call_target="tpu_custom_call" | custom-call | tf_op jit(solution)/shard_map/search/pallas_call | solution.py:233
Async XLA Ops:
  0.0 0.7 %copy-start.2 = (s32[128]{0:T(128)S(1)}, s32[128]{0:T(128)}, u32[]{:S(2)}) copy-start(s32[128]{0:T(128)} %param.5) | copy-start | bytes 1540
  0.7 1.2 %copy-start = (bf16[2,256,1024]{2,1,0:T(8,128)(2,1)S(1)}, bf16[2,256,1024]{2,1,0:T(8,128)(2,1)}, u32[]{:S(2)}) copy-start(bf16[2,256,1024]{2,1,0:T(8,128)(2,1)} %bank_ref.1) | copy-start | bytes 3145732
  1.9 0.7 %copy-start.1 = (bf16[2,2048]{1,0:T(2,128)(2,1)S(1)}, bf16[2,2048]{1,0:T(2,128)(2,1)}, u32[]{:S(2)}) copy-start(bf16[2,2048]{1,0:T(2,128)(2,1)} %spec_ref.1) | copy-start | bytes 24580

commit v2 on v1

--- a/solution.py
+++ b/solution.py
@@ -48,12 +48,14 @@
     return found
 
 
-def gather_kernel(plan, spec_ref, index_ref, bank_ref, win_ref, lhs_ref, bank, bank_sem, send_sems, recv_sems):
+def gather_kernel(plan, spec_ref, index_ref, bank_ref, win_ref, lhs_ref, bank, index, bank_sem, index_sem, send_sems, recv_sems):
     me = lax.axis_index("freq")
     size = plan.granule
     rows = plan.rows
     fetch = pltpu.make_async_copy(bank_ref, bank, bank_sem)
     fetch.start()
+    fetch_index = pltpu.make_async_copy(index_ref, index, index_sem)
+    fetch_index.start()
     barrier = pltpu.get_barrier_semaphore()
 
     def greet(step, carry):
@@ -102,9 +104,10 @@
 
     each(lambda copy: copy.start(), lambda copy: copy.start())
 
+    fetch_index.wait()
     fetch.wait()
     names = lax.broadcasted_iota(jnp.int32, (bank.shape[1], rows), 0)
-    picks = (names == index_ref[...]).astype(jnp.float32).T.astype(jnp.bfloat16)
+    picks = (names == index[...]).astype(jnp.float32).T.astype(jnp.bfloat16)
     real = jnp.dot(picks, bank[0], preferred_element_type=jnp.float32).astype(jnp.bfloat16)
     imag = jnp.dot(picks, bank[1], preferred_element_type=jnp.float32).astype(jnp.bfloat16)
     lhs_ref[0, :rows] = real
@@ -134,73 +137,97 @@
     return make(left, right).astype(jnp.float32).astype(jnp.bfloat16)
 
 
-def search_kernel(plan, win_ref, lhs_ref, out_ref, shifts_re, shifts_im, half_ref, quarter_ref, three_ref):
+def search_kernel(plan, win_ref, lhs_ref, out_ref, *scratch):
     rows, taps = plan.rows, plan.taps
-    width = plan.width
-    blocks = width // LANES
-
-    for which, shifts in ((0, shifts_re), (1, shifts_im)):
-        base = jnp.broadcast_to(win_ref[which : which + 1, :].astype(jnp.float32), (16, width))
-        place = lax.broadcasted_iota(jnp.int32, (16, width), 0)
-        for bit in (1, 2, 4, 8):
-            base = jnp.where((place & bit) != 0, pltpu.roll(base, width - bit, 1), base)
-        base = base.astype(jnp.bfloat16)
-        for turn in range(LANES // 16):
+    parts = len(RATIOS)
+    shifts, held = scratch[: 2 * parts], scratch[2 * parts :]
+
+    def build(part):
+        width = plan.part_cols[part] + taps
+        start = plan.offsets[part]
+        bases = []
+
+        def first(which):
+            line = win_ref[which : which + 1, start : start + width].astype(jnp.float32)
+            base = jnp.broadcast_to(line, (8, width))
+            place = lax.broadcasted_iota(jnp.int32, (8, width), 0)
+            for bit in (1, 2, 4):
+                base = jnp.where((place & bit) != 0, pltpu.roll(base, width - bit, 1), base)
+            base = jnp.concatenate([base, pltpu.roll(base, width - 8, 1)], 0)
+            bases.append(base.astype(jnp.bfloat16))
+
+        def turned(which, turn):
+            base = bases[which]
+            into = shifts[2 * part + which]
             moved = base if turn == 0 else pltpu.roll(base, width - 16 * turn, 1)
-            for block in range(blocks):
+            for block in range(width // LANES):
                 piece = moved[:, block * LANES : (block + 1) * LANES]
                 spot = block * LANES + 16 * turn
-                shifts[spot : spot + 16, 0:LANES] = piece
+                into[spot : spot + 16, 0:LANES] = piece
                 if block:
-                    shifts[spot - LANES : spot - LANES + 16, LANES : 2 * LANES] = piece
+                    into[spot - LANES : spot - LANES + 16, LANES : 2 * LANES] = piece
+
+        tasks = [functools.partial(first, which) for which in (0, 1)]
+        tasks += [functools.partial(turned, which, turn) for turn in range(LANES // 16) for which in (0, 1)]
+        return tasks
 
     def power(part, chunk):
         count = plan.part_rows[part]
-        start = pl.multiple_of(plan.offsets[part] + chunk * CHUNK, CHUNK)
+        start = chunk * CHUNK
 
         def left(which):
             if count == rows:
                 return lhs_ref[which]
             return jnp.concatenate([lhs_ref[which, :count], lhs_ref[which, rows : rows + count]], 0)
 
-        both = jnp.dot(left(0), shifts_re[pl.ds(start, taps), :], preferred_element_type=jnp.float32)
-        both += jnp.dot(left(1), shifts_im[pl.ds(start, taps), :], preferred_element_type=jnp.float32)
+        both = sum(
+            jnp.dot(left(which), shifts[2 * part + which][start : start + taps, :], preferred_element_type=jnp.float32)
+            for which in (0, 1)
+        )
         real, imag = both[:count], both[count:]
         return (real * real + imag * imag).astype(jnp.bfloat16)
 
-    for part, held in ((1, half_ref), (2, quarter_ref), (3, three_ref)):
+    def fill(part, chunk):
         n, d = RATIOS[part]
         spread = one_hot((rows, plan.part_rows[part]), lambda z, k: z * n // d == k)
-
-        def fill(chunk, carry):
-            cells = jnp.dot(spread, power(part, chunk), preferred_element_type=jnp.float32)
-            held[:, pl.ds(pl.multiple_of(chunk * CHUNK, CHUNK), CHUNK)] = cells.astype(jnp.bfloat16)
-            return carry
-
-        lax.fori_loop(0, plan.part_cols[part] // CHUNK, fill, 0)
+        cells = jnp.dot(spread, power(part, chunk), preferred_element_type=jnp.float32)
+        held[part - 1][:, chunk * CHUNK : (chunk + 1) * CHUNK] = cells.astype(jnp.bfloat16)
 
     half = one_hot((LANES, CHUNK), lambda k, r: k == r // 2)
     quarters = [one_hot((LANES, CHUNK), lambda k, r: k == CHUNK // 4 * odd + r // 4) for odd in (0, 1)]
     threes = [one_hot((CHUNK, CHUNK), lambda k, r: k == CHUNK // 4 * odd + 3 * r // 4) for odd in (0, 1)]
-    spreads = [jnp.concatenate([half, quarters[odd], threes[odd]], 0) for odd in (0, 1)]
-
-    def pair(step, carry):
-        for odd in (0, 1):
-            chunk = 2 * step + odd
-            total = power(0, chunk).astype(jnp.float32)
-            cells = jnp.concatenate(
-                [
-                    half_ref[:, pl.ds(pl.multiple_of(chunk * LANES, LANES), LANES)],
-                    quarter_ref[:, pl.ds(pl.multiple_of(step * LANES, LANES), LANES)],
-                    three_ref[:, pl.ds(pl.multiple_of(step * 3 * LANES + odd * LANES, LANES), CHUNK)],
-                ],
-                1,
-            )
-            total += jnp.dot(cells, spreads[odd], preferred_element_type=jnp.float32)
-            out_ref[:, pl.ds(pl.multiple_of(chunk * CHUNK, CHUNK), CHUNK)] = total
-        return carry
-
-    lax.fori_loop(0, plan.cols // (2 * CHUNK), pair, 0)
+
+    def finish(chunk):
+        step, odd = divmod(chunk, 2)
+        total = power(0, chunk).astype(jnp.float32)
+        spots = (
+            (held[0], chunk * LANES, half),
+            (held[1], step * LANES, quarters[odd]),
+            (held[2], (3 * step + odd) * LANES, threes[odd]),
+        )
+        cells = jnp.concatenate([ref[:, at : at + spread.shape[0]] for ref, at, spread in spots], 1)
+        spreads = jnp.concatenate([spread for _, _, spread in spots], 0)
+        total += jnp.dot(cells, spreads, preferred_element_type=jnp.float32)
+        out_ref[:, chunk * CHUNK : (chunk + 1) * CHUNK] = total
+
+    def run(products, builds):
+        done = 0
+        for number, product in enumerate(products):
+            product()
+            until = len(builds) * (number + 1) // len(products)
+            for task in builds[done:until]:
+                task()
+            done = until
+
+    def fills(part):
+        return [functools.partial(fill, part, chunk) for chunk in range(plan.part_cols[part] // CHUNK)]
+
+    for task in build(2):
+        task()
+    run(fills(2), build(1))
+    run(fills(1), build(3))
+    run(fills(3), build(0))
+    run([functools.partial(finish, chunk) for chunk in range(plan.cols // CHUNK)], [])
 
 
 def body(spectrum, template_bank, template_index):
@@ -217,10 +244,12 @@
             jax.ShapeDtypeStruct((2, plan.width), jnp.bfloat16),
             jax.ShapeDtypeStruct((2, 2 * rows, taps), jnp.bfloat16),
         ),
-        in_specs=[pl.BlockSpec(memory_space=pl.ANY), vmem, pl.BlockSpec(memory_space=pl.ANY)],
+        in_specs=[pl.BlockSpec(memory_space=pltpu.HBM)] * 3,
         out_specs=(vmem, vmem),
         scratch_shapes=[
             pltpu.VMEM(template_bank.shape, jnp.bfloat16),
+            pltpu.VMEM((1, rows), jnp.int32),
+            pltpu.SemaphoreType.DMA,
             pltpu.SemaphoreType.DMA,
             pltpu.SemaphoreType.DMA((send_count,)),
             pltpu.SemaphoreType.DMA((plan.slot_count,)),
@@ -236,11 +265,8 @@
         in_specs=[vmem, vmem],
         out_specs=vmem,
         scratch_shapes=[
-            pltpu.VMEM((plan.width, CHUNK), jnp.bfloat16),
-            pltpu.VMEM((plan.width, CHUNK), jnp.bfloat16),
-            pltpu.VMEM((rows, plan.part_cols[1]), jnp.bfloat16),
-            pltpu.VMEM((rows, plan.part_cols[2]), jnp.bfloat16),
-            pltpu.VMEM((rows, plan.part_cols[3]), jnp.bfloat16),
+            *[pltpu.VMEM((width + taps, CHUNK), jnp.bfloat16) for width in plan.part_cols for _ in range(2)],
+            *[pltpu.VMEM((rows, width), jnp.bfloat16) for width in plan.part_cols[1:]],
         ],
         compiler_params=pltpu.CompilerParams(vmem_limit_bytes=32 << 20),
         name="search",

time: 23.4 us -> 22.7 us (0.970)
  Pallas kernels: 20.6 us -> 19.9 us
    pallas_call x1, Pallas kernels: 12.4 us -> 11.6 us  [body(): pl.pallas_call(functools.partial(search_kernel, plan), out_shape=jax.Shap...]
where the time goes in v2:
time: 22.7 us; the launch traced here: 22.4 us
  Pallas kernels  19.9 us (88%)
  local copies, waits for them, and re-layouts  2.58 us (11%)
    pallas_call x1, Pallas kernels, body(): pl.pallas_call(functools.partial(search_kernel, plan), out_shape=jax.Shap...  11.6 us
    pallas_call x1, Pallas kernels, body(): pl.pallas_call(functools.partial(gather_kernel, plan), out_shape=(jax.Sha...  8.22 us
    unnamed x6, local copies, waits for them, and re-layouts  2.58 us

profile of v2, /device:TPU:1, one launch (start us, length us, event | category | flops | bytes accessed | tf_op | source)
XLA Modules:
  0.0 22.4 jit_solution(10374431292178988538)
XLA Ops:
  0.0 0.0 copy-start.2
  0.0 0.7 %copy-done.2 = s32[128]{0:T(128)S(1)} copy-done((s32[128]{0:T(128)S(1)}, s32[128]{0:T(128)}, u32[]{:S(2)}) %copy-start.2) | copy-done | bytes 536
  0.7 0.0 copy-start
  0.7 1.2 %copy-done = bf16[2,256,1024]{2,1,0:T(8,128)(2,1)S(1)} copy-done((bf16[2,256,1024]{2,1,0:T(8,128)(2,1)S(1)}, bf16[2,256,1024]{2,1,0:T(8,128)(2,1)}, u32[]{:S(2)}) %copy-start) | copy-done | bytes 1048600
  1.9 0.0 copy-start.1
  1.9 0.7 %copy-done.1 = bf16[2,2048]{1,0:T(2,128)(2,1)S(1)} copy-done((bf16[2,2048]{1,0:T(2,128)(2,1)S(1)}, bf16[2,2048]{1,0:T(2,128)(2,1)}, u32[]{:S(2)}) %copy-start.1) | copy-done | bytes 8216
  2.6 8.2 %gather.1 = (bf16[2,9216]{1,0:T(2,128)(2,1)S(1)}, bf16[2,256,1024]{2,1,0:T(8,128)(2,1)S(1)}) custom-call(bf16[2,2048]{1,0:T(2,128)(2,1)S(1)} %copy-done.1, s32[1,128]{1,0:T(1,128)S(1)} %bitcast.1, bf16[2,256,1024]{2,1,0:T(8,128)(2,1)S(1)} %copy-done), custom_call_target="tpu_custom_call" | custom-call | tf_op jit(solution)/shard_map/gather/pallas_call | solution.py:241
  10.8 11.6 %search.1 = f32[128,2048]{1,0:T(8,128)} custom-call(bf16[2,9216]{1,0:T(2,128)(2,1)S(1)} %get-tuple-element.7.win_ref, bf16[2,256,1024]{2,1,0:T(8,128)(2,1)S(1)} %get-tuple-element.8.lhs_ref), custom_call_target="tpu_custom_call" | custom-call | tf_op jit(solution)/shard_map/search/pallas_call | solution.py:262
Async XLA Ops:
  0.0 0.7 %copy-start.2 = (s32[128]{0:T(128)S(1)}, s32[128]{0:T(128)}, u32[]{:S(2)}) copy-start(s32[128]{0:T(128)} %param.5) | copy-start | bytes 1540
  0.7 1.2 %copy-start = (bf16[2,256,1024]{2,1,0:T(8,128)(2,1)S(1)}, bf16[2,256,1024]{2,1,0:T(8,128)(2,1)}, u32[]{:S(2)}) copy-start(bf16[2,256,1024]{2,1,0:T(8,128)(2,1)} %bank_ref.1) | copy-start | bytes 3145732
  1.9 0.7 %copy-start.1 = (bf16[2,2048]{1,0:T(2,128)(2,1)S(1)}, bf16[2,2048]{1,0:T(2,128)(2,1)}, u32[]{:S(2)}) copy-start(bf16[2,2048]{1,0:T(2,128)(2,1)} %spec_ref.1) | copy-start | bytes 24580

commit v3 on v2

v3 whole, which is shorter than its diff:
```python
import functools

import jax
import jax.numpy as jnp
from jax import lax
from jax.experimental import pallas as pl
from jax.experimental.pallas import tpu as pltpu
from jax.sharding import PartitionSpec as P

RATIOS = ((1, 1), (1, 2), (1, 4), (3, 4))
CHUNK = 256
LANES = 128


class Plan:
    def __init__(self, cols, taps, rows, owners):
        self.cols, self.taps, self.rows, self.owners = cols, taps, rows, owners
        self.granule = taps // 2
        self.held = cols // self.granule
        self.steps = [self.held * n // d for n, d in RATIOS]
        self.part_cols = [cols * n // d for n, d in RATIOS]
        self.part_rows = [rows * n // d for n, d in RATIOS]
        self.offsets, self.slots = [], []
        offset = slot = 0
        for width in self.part_cols:
            self.offsets.append(offset)
            self.slots.append(slot)
            offset += width + taps
            slot += (width + taps) // self.granule
        self.width, self.slot_count = offset, slot


def sends(plan, me):
    found = []
    for own in range(plan.held):
        for part, step in enumerate(plan.steps):
            spot = plan.held * me + own + 1
            last = spot // step
            rest = spot - last * step
            for back in range((step + 1) // step + 1):
                if plan.held % step == 0:
                    if (own + 1) % step + step * back >= step + 2:
                        continue
                to = last - back
                place = rest + step * back
                fits = (to >= 0) & (to < plan.owners) & (place < step + 2)
                found.append((own, part, to, place, fits))
    return found


def one_hot(shape, make):
    left = lax.broadcasted_iota(jnp.int32, shape, 0)
    right = lax.broadcasted_iota(jnp.int32, shape, 1)
    return make(left, right).astype(jnp.float32).astype(jnp.bfloat16)


def search_kernel(plan, spec_ref, index_ref, bank_ref, out_ref, win, bank, index, lhs, plane, *scratch):
    rows, taps, size = plan.rows, plan.taps, plan.granule
    parts = len(RATIOS)
    shifts, held = scratch[: 2 * parts], scratch[2 * parts : 3 * parts - 1]
    bank_sem, index_sem, own_sem, send_sems, recv_sems = scratch[3 * parts - 1 :]
    me = lax.axis_index("freq")

    own_start = plan.offsets[0] + size
    fetch_own = pltpu.make_async_copy(spec_ref, win.at[:, own_start : own_start + plan.cols], own_sem)
    fetch_own.start()
    fetch_index = pltpu.make_async_copy(index_ref, index, index_sem)
    fetch_index.start()
    fetch_bank = pltpu.make_async_copy(bank_ref, bank, bank_sem)
    fetch_bank.start()

    barrier = pltpu.get_barrier_semaphore()

    def greet(step, carry):
        peer = lax.rem(me + step, plan.owners)
        pl.semaphore_signal(barrier, inc=1, device_id={"freq": peer}, device_id_type=pl.DeviceIdType.MESH)
        return carry

    lax.fori_loop(1, plan.owners, greet, 0)

    @pl.when(me == 0)
    def _():
        for offset in plan.offsets:
            win[:, offset : offset + size] = jnp.zeros((2, size), win.dtype)

    @pl.when(me == plan.owners - 1)
    def _():
        end = plan.offsets[0] + plan.part_cols[0] + plan.taps
        win[:, end - size : end] = jnp.zeros((2, size), win.dtype)

    def each(act_remote, act_local):
        for number, (own, part, to, place, fits) in enumerate(sends(plan, me)):
            source = spec_ref.at[:, own * size : (own + 1) * size]
            target = win.at[:, pl.ds(pl.multiple_of(plan.offsets[part] + place * size, size), size)]
            got = recv_sems.at[plan.slots[part] + place]

            @pl.when(fits & (to != me))
            def _():
                act_remote(
                    pltpu.make_async_remote_copy(
                        src_ref=source,
                        dst_ref=target,
                        send_sem=send_sems.at[number],
                        recv_sem=got,
                        device_id={"freq": to},
                        device_id_type=pl.DeviceIdType.MESH,
                    )
                )

            if act_local is not None and part:

                @pl.when(fits & (to == me))
                def _():
                    act_local(pltpu.make_async_copy(source, target, got))

    def receive(part):
        step = plan.steps[part]
        for place in range(step + 2):
            if part == 0 and 0 < place <= plan.held:
                continue
            spot = step * me - 1 + place

            @pl.when((spot >= 0) & (spot < plan.held * plan.owners))
            def _():
                start = plan.offsets[part] + place * size
                pltpu.make_async_copy(
                    spec_ref.at[:, 0:size],
                    win.at[:, start : start + size],
                    recv_sems.at[plan.slots[part] + place],
                ).wait()

    def build(part, low, high):
        width = (high - low + 1) * LANES
        start = plan.offsets[part] + low * LANES
        bases = []

        def first(which):
            line = win[which : which + 1, start : start + width].astype(jnp.float32)
            base = jnp.broadcast_to(line, (8, width))
            place = lax.broadcasted_iota(jnp.int32, (8, width), 0)
            for bit in (1, 2, 4):
                base = jnp.where((place & bit) != 0, pltpu.roll(base, width - bit, 1), base)
            base = jnp.concatenate([base, pltpu.roll(base, width - 8, 1)], 0)
            bases.append(base.astype(jnp.bfloat16))

        def turned(which, turn):
            base = bases[which]
            into = shifts[2 * part + which]
            moved = base if turn == 0 else pltpu.roll(base, width - 16 * turn, 1)
            for block in range(high - low):
                piece = moved[:, block * LANES : (block + 1) * LANES]
                spot = (low + block) * LANES + 16 * turn
                into[spot : spot + 16, 0:LANES] = piece
                if spot >= LANES:
                    into[spot - LANES : spot - LANES + 16, LANES : 2 * LANES] = piece

        tasks = [functools.partial(first, which) for which in (0, 1)]
        tasks += [functools.partial(turned, which, turn) for turn in range(LANES // 16) for which in (0, 1)]
        return tasks

    def power(part, chunk):
        count = plan.part_rows[part]
        start = chunk * CHUNK
        if count == rows:
            left = lhs[...]
        else:
            left = jnp.concatenate([lhs[:count], lhs[rows : rows + count]], 0)
        right = jnp.concatenate([shifts[2 * part + which][start : start + taps, :] for which in (0, 1)], 0)
        both = jnp.dot(left, right, preferred_element_type=jnp.float32)
        real, imag = both[:count], both[count:]
        return (real * real + imag * imag).astype(jnp.bfloat16)

    def keep(chunk):
        plane[:, chunk * CHUNK : (chunk + 1) * CHUNK] = power(0, chunk)

    def fill(part, chunk):
        n, d = RATIOS[part]
        spread = one_hot((rows, plan.part_rows[part]), lambda z, k: z * n // d == k)
        cells = jnp.dot(spread, power(part, chunk), preferred_element_type=jnp.float32)
        held[part - 1][:, chunk * CHUNK : (chunk + 1) * CHUNK] = cells.astype(jnp.bfloat16)

    def finish(chunk):
        half = one_hot((LANES, CHUNK), lambda k, r: k == r // 2)
        quarters = [one_hot((LANES, CHUNK), lambda k, r: k == CHUNK // 4 * odd + r // 4) for odd in (0, 1)]
        threes = [one_hot((CHUNK, CHUNK), lambda k, r: k == CHUNK // 4 * odd + 3 * r // 4) for odd in (0, 1)]
        step, odd = divmod(chunk, 2)
        spots = (
            (held[0], chunk * LANES, half),
            (held[1], step * LANES, quarters[odd]),
            (held[2], (3 * step + odd) * LANES, threes[odd]),
        )
        cells = jnp.concatenate([ref[:, at : at + spread.shape[0]] for ref, at, spread in spots], 1)
        spreads = jnp.concatenate([spread for _, _, spread in spots], 0)
        total = plane[:, chunk * CHUNK : (chunk + 1) * CHUNK].astype(jnp.float32)
        total += jnp.dot(cells, spreads, preferred_element_type=jnp.float32)
        out_ref[:, chunk * CHUNK : (chunk + 1) * CHUNK] = total

    def run(products, builds):
        done = 0
        for number, product in enumerate(products):
            product()
            until = len(builds) * (number + 1) // len(products)
            for task in builds[done:until]:
                task()
            done = until

    def fills(part):
        return [functools.partial(fill, part, chunk) for chunk in range(plan.part_cols[part] // CHUNK)]

    def whole(part):
        return build(part, 0, (plan.part_cols[part] + taps) // LANES - 1)

    halo = size // LANES
    last = (plan.cols + taps) // LANES - 1

    fetch_own.wait()
    for task in build(0, halo, last - halo):
        task()
    pl.semaphore_wait(barrier, plan.owners - 1)
    each(lambda copy: copy.start(), lambda copy: copy.start())

    fetch_index.wait()
    fetch_bank.wait()
    names = lax.broadcasted_iota(jnp.int32, (bank.shape[1], rows), 0)
    picks = (names == index[...]).astype(jnp.float32).T.astype(jnp.bfloat16)
    real = jnp.dot(picks, bank[0], preferred_element_type=jnp.float32).astype(jnp.bfloat16)
    imag = jnp.dot(picks, bank[1], preferred_element_type=jnp.float32).astype(jnp.bfloat16)
    lhs[:rows, :taps] = real
    lhs[rows:, :taps] = imag
    lhs[:rows, taps:] = -imag
    lhs[rows:, taps:] = real

    chunks = plan.cols // CHUNK
    edge = size // CHUNK
    for chunk in range(edge, chunks - edge):
        keep(chunk)
    receive(0)
    for task in build(0, 0, halo) + build(0, last - halo, last):
        task()
    for chunk in [*range(edge), *range(chunks - edge, chunks)]:
        keep(chunk)
    for part in range(1, parts):
        receive(part)
    for task in whole(2):
        task()
    run(fills(2), whole(1))
    run(fills(1), whole(3))
    run(fills(3), [])
    for chunk in range(chunks):
        finish(chunk)

    each(lambda copy: copy.wait_send(), None)


def body(spectrum, template_bank, template_index):
    owners = lax.axis_size("freq")
    taps = template_bank.shape[2]
    rows = template_index.shape[0]
    cols = spectrum.shape[1]
    plan = Plan(cols, taps, rows, owners)
    send_count = len(sends(plan, 0))
    return pl.pallas_call(
        functools.partial(search_kernel, plan),
        out_shape=jax.ShapeDtypeStruct((rows, cols), jnp.float32),
        in_specs=[pl.BlockSpec(memory_space=pl.ANY)] * 3,
        out_specs=pl.BlockSpec(memory_space=pltpu.VMEM),
        scratch_shapes=[
            pltpu.VMEM((2, plan.width), jnp.bfloat16),
            pltpu.VMEM(template_bank.shape, jnp.bfloat16),
            pltpu.VMEM((1, rows), jnp.int32),
            pltpu.VMEM((2 * rows, 2 * taps), jnp.bfloat16),
            pltpu.VMEM((rows, cols), jnp.bfloat16),
            *[pltpu.VMEM((width + taps, CHUNK), jnp.bfloat16) for width in plan.part_cols for _ in range(2)],
            *[pltpu.VMEM((rows, width), jnp.bfloat16) for width in plan.part_cols[1:]],
            pltpu.SemaphoreType.DMA,
            pltpu.SemaphoreType.DMA,
            pltpu.SemaphoreType.DMA,
            pltpu.SemaphoreType.DMA((send_count,)),
            pltpu.SemaphoreType.DMA((plan.slot_count,)),
        ],
        compiler_params=pltpu.CompilerParams(collective_id=0, has_side_effects=True),
        name="search",
    )(spectrum, template_index.reshape(1, rows), template_bank)


def solution(mesh):
    return jax.shard_map(
        body,
        mesh=mesh,
        in_specs=(P(None, ("beam", "freq")), P(), P()),
        out_specs=P(None, ("beam", "freq")),
        check_vma=False,
    )
```

time: 22.7 us -> 21.2 us (0.934)
  Pallas kernels: 19.9 us -> 18.7 us
  local copies, waits for them, and re-layouts: 2.58 us -> 2.3 us
    pallas_call x1 -> x0, Pallas kernels: 8.22 us -> none  [body(): pl.pallas_call(functools.partial(gather_kernel, plan), out_shape=(jax.Sha...]
    pallas_call x1, Pallas kernels: 11.6 us -> 18.7 us  [body(): pl.pallas_call(functools.partial(search_kernel, plan), out_shape=jax.Shap...]
    unnamed x6 -> x1, local copies, waits for them, and re-layouts: 2.58 us -> 2.3 us
where the time goes in v3:
time: 21.2 us; the launch traced here: 21 us
  Pallas kernels  18.7 us (88%)
  local copies, waits for them, and re-layouts  2.3 us (11%)
    pallas_call x1, Pallas kernels, body(): pl.pallas_call(functools.partial(search_kernel, plan), out_shape=jax.Shap...  18.7 us
    unnamed x1, local copies, waits for them, and re-layouts  2.3 us

profile of v3, /device:TPU:1, one launch (start us, length us, event | category | flops | bytes accessed | tf_op | source)
XLA Modules:
  0.0 21.0 jit_solution(7270317869621500392)
XLA Ops:
  0.0 18.7 %search.1 = f32[128,2048]{1,0:T(8,128)} custom-call(bf16[2,2048]{1,0:T(2,128)(2,1)} %spec_ref.1, s32[1,128]{1,0:T(1,128)} %bitcast.1, bf16[2,256,1024]{2,1,0:T(8,128)(2,1)} %bank_ref.1), custom_call_target="tpu_custom_call" | custom-call | tf_op jit(solution)/shard_map/search/pallas_call | solution.py:262
  18.7 2.3 %copy.5 = f32[128,2048]{1,0:T(8,128)} copy(f32[128,2048]{1,0:T(8,128)} %search.1) | data formatting | bytes 2097152

commit v4 on v3

v4 whole, which is shorter than its diff:
```python
import functools

import jax
import jax.numpy as jnp
from jax import lax
from jax.experimental import pallas as pl
from jax.experimental.pallas import tpu as pltpu
from jax.sharding import PartitionSpec as P

RATIOS = ((1, 1), (1, 2), (1, 4), (3, 4))
CHUNK = 256
LANES = 128


class Plan:
    def __init__(self, cols, taps, rows, owners):
        self.cols, self.taps, self.rows, self.owners = cols, taps, rows, owners
        self.granule = taps // 2
        self.held = cols // self.granule
        self.steps = [self.held * n // d for n, d in RATIOS]
        self.part_cols = [cols * n // d for n, d in RATIOS]
        self.part_rows = [rows * n // d for n, d in RATIOS]
        self.offsets, self.slots = [], []
        offset = slot = 0
        for width in self.part_cols:
            self.offsets.append(offset)
            self.slots.append(slot)
            offset += width + taps if self.offsets[1:] else 0
            slot += (width + taps) // self.granule
        self.width, self.slot_count = offset, slot


def sends(plan, me):
    found = []
    for own in range(plan.held):
        for part, step in enumerate(plan.steps):
            spot = plan.held * me + own + 1
            last = spot // step
            rest = spot - last * step
            for back in range((step + 1) // step + 1):
                if plan.held % step == 0:
                    if (own + 1) % step + step * back >= step + 2:
                        continue
                to = last - back
                place = rest + step * back
                fits = (to >= 0) & (to < plan.owners) & (place < step + 2)
                found.append((own, part, to, place, fits))
    return found


def one_hot(shape, make):
    left = lax.broadcasted_iota(jnp.int32, shape, 0)
    right = lax.broadcasted_iota(jnp.int32, shape, 1)
    return make(left, right).astype(jnp.float32).astype(jnp.bfloat16)


def build(window, shifts, low, high):
    width = (high - low + 1) * LANES
    start = low * LANES
    bases = []

    def first(which):
        line = window[which : which + 1, start : start + width].astype(jnp.float32)
        base = jnp.broadcast_to(line, (8, width))
        place = lax.broadcasted_iota(jnp.int32, (8, width), 0)
        for bit in (1, 2, 4):
            base = jnp.where((place & bit) != 0, pltpu.roll(base, width - bit, 1), base)
        base = jnp.concatenate([base, pltpu.roll(base, width - 8, 1)], 0)
        bases.append(base.astype(jnp.bfloat16))

    def turned(which, turn):
        base = bases[which]
        into = shifts[which]
        moved = base if turn == 0 else pltpu.roll(base, width - 16 * turn, 1)
        for block in range(high - low):
            piece = moved[:, block * LANES : (block + 1) * LANES]
            spot = (low + block) * LANES + 16 * turn
            into[spot : spot + 16, 0:LANES] = piece
            if spot >= LANES:
                into[spot - LANES : spot - LANES + 16, LANES : 2 * LANES] = piece

    tasks = [functools.partial(first, which) for which in (0, 1)]
    tasks += [functools.partial(turned, which, turn) for turn in range(LANES // 16) for which in (0, 1)]
    return tasks


def power(lhs, shifts, count, taps, start, width):
    rows = lhs.shape[0] // 2
    if count == rows:
        left = lhs[...]
    else:
        left = jnp.concatenate([lhs[:count], lhs[rows : rows + count]], 0)
    right = jnp.concatenate(
        [
            jnp.concatenate(
                [shifts[which][start + at : start + at + taps, :] for at in range(0, width, CHUNK)], 1
            )
            for which in (0, 1)
        ],
        0,
    )
    both = jnp.dot(left, right, preferred_element_type=jnp.float32)
    real, imag = both[:count], both[count:]
    return (real * real + imag * imag).astype(jnp.bfloat16)


def gather_kernel(plan, spec_ref, index_ref, bank_ref, win_out, lhs_out, plane_out, win, bank, index, lhs, plane, *scratch):
    rows, taps, size = plan.rows, plan.taps, plan.granule
    parts = len(RATIOS)
    shifts = scratch[:2]
    bank_sem, index_sem, own_sem, out_sems, send_sems, recv_sems = scratch[2:]
    me = lax.axis_index("freq")

    own_start = size
    fetch_own = pltpu.make_async_copy(spec_ref, win.at[:, own_start : own_start + plan.cols], own_sem)
    fetch_own.start()
    fetch_index = pltpu.make_async_copy(index_ref, index, index_sem)
    fetch_index.start()
    fetch_bank = pltpu.make_async_copy(bank_ref, bank, bank_sem)
    fetch_bank.start()

    barrier = pltpu.get_barrier_semaphore()

    def greet(step, carry):
        peer = lax.rem(me + step, plan.owners)
        pl.semaphore_signal(barrier, inc=1, device_id={"freq": peer}, device_id_type=pl.DeviceIdType.MESH)
        return carry

    lax.fori_loop(1, plan.owners, greet, 0)

    @pl.when(me == 0)
    def _():
        win[:, 0:size] = jnp.zeros((2, size), win.dtype)

    @pl.when(me == plan.owners - 1)
    def _():
        end = plan.cols + plan.taps
        win[:, end - size : end] = jnp.zeros((2, size), win.dtype)

    def each(act_remote, act_local):
        for number, (own, part, to, place, fits) in enumerate(sends(plan, me)):
            source = spec_ref.at[:, own * size : (own + 1) * size]
            into = win if part == 0 else win_out
            target = into.at[:, pl.ds(pl.multiple_of(plan.offsets[part] + place * size, size), size)]
            got = recv_sems.at[plan.slots[part] + place]

            @pl.when(fits & (to != me))
            def _():
                act_remote(
                    pltpu.make_async_remote_copy(
                        src_ref=source,
                        dst_ref=target,
                        send_sem=send_sems.at[number],
                        recv_sem=got,
                        device_id={"freq": to},
                        device_id_type=pl.DeviceIdType.MESH,
                    )
                )

            if act_local is not None and part:

                @pl.when(fits & (to == me))
                def _():
                    act_local(pltpu.make_async_copy(source, target, got))

    def receive(part):
        step = plan.steps[part]
        for place in range(step + 2):
            if part == 0 and 0 < place <= plan.held:
                continue
            spot = step * me - 1 + place

            def land():
                start = plan.offsets[part] + place * size
                pltpu.make_async_copy(
                    spec_ref.at[:, 0:size],
                    (win if part == 0 else win_out).at[:, start : start + size],
                    recv_sems.at[plan.slots[part] + place],
                ).wait()

            if part:
                land()
            else:
                pl.when((spot >= 0) & (spot < plan.held * plan.owners))(land)

    def keep(chunk):
        plane[:, chunk * CHUNK : (chunk + 1) * CHUNK] = power(lhs, shifts, rows, taps, chunk * CHUNK, CHUNK)

    halo = size // LANES
    last = (plan.cols + taps) // LANES - 1

    fetch_own.wait()
    for task in build(win, shifts, halo, last - halo):
        task()
    pl.semaphore_wait(barrier, plan.owners - 1)
    each(lambda copy: copy.start(), lambda copy: copy.start())

    @pl.when(me == 0)
    def _():
        for part in range(1, parts):
            start = plan.offsets[part]
            pltpu.make_async_copy(
                win.at[:, 0:size], win_out.at[:, start : start + size], recv_sems.at[plan.slots[part]]
            ).start()

    fetch_index.wait()
    fetch_bank.wait()
    names = lax.broadcasted_iota(jnp.int32, (bank.shape[1], rows), 0)
    picks = (names == index[...]).astype(jnp.float32).T.astype(jnp.bfloat16)
    real = jnp.dot(picks, bank[0], preferred_element_type=jnp.float32).astype(jnp.bfloat16)
    imag = jnp.dot(picks, bank[1], preferred_element_type=jnp.float32).astype(jnp.bfloat16)
    lhs[:rows, :taps] = real
    lhs[rows:, :taps] = imag
    lhs[:rows, taps:] = -imag
    lhs[rows:, taps:] = real

    chunks = plan.cols // CHUNK
    edge = size // CHUNK
    for chunk in range(edge, chunks - edge):
        keep(chunk)
    put_lhs = pltpu.make_async_copy(lhs, lhs_out, out_sems.at[0])
    put_lhs.start()
    receive(0)
    for task in build(win, shifts, 0, halo) + build(win, shifts, last - halo, last):
        task()
    for chunk in [*range(edge), *range(chunks - edge, chunks)]:
        keep(chunk)
    put_plane = pltpu.make_async_copy(plane, plane_out, out_sems.at[1])
    put_plane.start()
    for part in range(1, parts):
        receive(part)
    put_lhs.wait()
    put_plane.wait()
    each(lambda copy: copy.wait_send(), None)


def search_kernel(plan, win_ref, lhs_ref, plane_ref, out_ref, win, lhs, plane, out, *scratch):
    rows, taps = plan.rows, plan.taps
    parts = len(RATIOS)
    shifts, held = scratch[: 2 * parts - 2], scratch[2 * parts - 2 : 3 * parts - 3]
    in_sems, out_sems = scratch[3 * parts - 3 :]
    offsets = plan.offsets
    fetch_win = pltpu.make_async_copy(win_ref, win, in_sems.at[0])
    fetch_lhs = pltpu.make_async_copy(lhs_ref, lhs, in_sems.at[1])
    fetch_plane = pltpu.make_async_copy(plane_ref, plane, in_sems.at[2])
    fetch_win.start()
    fetch_lhs.start()
    fetch_plane.start()

    def put(chunk):
        spot = slice(chunk * CHUNK, (chunk + 1) * CHUNK)
        return pltpu.make_async_copy(out.at[:, spot], out_ref.at[:, spot], out_sems.at[chunk])

    def fill(part, start):
        width = 2 * CHUNK
        n, d = RATIOS[part]
        spread = one_hot((rows, plan.part_rows[part]), lambda z, k: z * n // d == k)
        cells = jnp.dot(spread, power(lhs, shifts[2 * part - 2 : 2 * part], plan.part_rows[part], taps, start, width), preferred_element_type=jnp.float32)
        held[part - 1][:, start : start + width] = cells.astype(jnp.bfloat16)

    def finish(chunk):
        half = one_hot((LANES, CHUNK), lambda k, r: k == r // 2)
        quarters = [one_hot((LANES, CHUNK), lambda k, r: k == CHUNK // 4 * odd + r // 4) for odd in (0, 1)]
        threes = [one_hot((CHUNK, CHUNK), lambda k, r: k == CHUNK // 4 * odd + 3 * r // 4) for odd in (0, 1)]
        step, odd = divmod(chunk, 2)
        spots = (
            (held[0], chunk * LANES, half),
            (held[1], step * LANES, quarters[odd]),
            (held[2], (3 * step + odd) * LANES, threes[odd]),
        )
        cells = jnp.concatenate([ref[:, at : at + spread.shape[0]] for ref, at, spread in spots], 1)
        spreads = jnp.concatenate([spread for _, _, spread in spots], 0)
        total = plane[:, chunk * CHUNK : (chunk + 1) * CHUNK].astype(jnp.float32)
        total += jnp.dot(cells, spreads, preferred_element_type=jnp.float32)
        out[:, chunk * CHUNK : (chunk + 1) * CHUNK] = total
        put(chunk).start()

    def run(products, builds):
        done = 0
        for number, product in enumerate(products):
            product()
            until = len(builds) * (number + 1) // len(products)
            for task in builds[done:until]:
                task()
            done = until

    def fills(part):
        return [functools.partial(fill, part, start) for start in range(0, plan.part_cols[part], 2 * CHUNK)]

    def whole(part):
        return build(win.at[:, offsets[part] : offsets[part] + plan.part_cols[part] + taps], shifts[2 * part - 2 : 2 * part], 0, (plan.part_cols[part] + taps) // LANES - 1)

    fetch_win.wait()
    for task in whole(2):
        task()
    fetch_lhs.wait()
    run(fills(2), whole(1))
    run(fills(1), whole(3))
    run(fills(3), [])
    fetch_plane.wait()
    for chunk in range(plan.cols // CHUNK):
        finish(chunk)
    for chunk in range(plan.cols // CHUNK):
        put(chunk).wait()


def body(spectrum, template_bank, template_index):
    owners = lax.axis_size("freq")
    taps = template_bank.shape[2]
    rows = template_index.shape[0]
    cols = spectrum.shape[1]
    plan = Plan(cols, taps, rows, owners)
    hbm = pl.BlockSpec(memory_space=pl.ANY)
    between = (
        ((2, plan.width), jnp.bfloat16),
        ((2 * rows, 2 * taps), jnp.bfloat16),
        ((rows, cols), jnp.bfloat16),
    )
    windows, lhs, plane = pl.pallas_call(
        functools.partial(gather_kernel, plan),
        out_shape=tuple(jax.ShapeDtypeStruct(*item) for item in between),
        in_specs=[hbm] * 3,
        out_specs=(hbm,) * 3,
        scratch_shapes=[
            pltpu.VMEM((2, cols + taps), jnp.bfloat16),
            pltpu.VMEM(template_bank.shape, jnp.bfloat16),
            pltpu.VMEM((1, rows), jnp.int32),
            *[pltpu.VMEM(*item) for item in between[1:]],
            *[pltpu.VMEM((cols + taps, CHUNK), jnp.bfloat16) for _ in range(2)],
            pltpu.SemaphoreType.DMA,
            pltpu.SemaphoreType.DMA,
            pltpu.SemaphoreType.DMA,
            pltpu.SemaphoreType.DMA((2,)),
            pltpu.SemaphoreType.DMA((len(sends(plan, 0)),)),
            pltpu.SemaphoreType.DMA((plan.slot_count,)),
        ],
        compiler_params=pltpu.CompilerParams(collective_id=0, has_side_effects=True),
        name="gather",
    )(spectrum, template_index.reshape(1, rows), template_bank)
    return pl.pallas_call(
        functools.partial(search_kernel, plan),
        out_shape=jax.ShapeDtypeStruct((rows, cols), jnp.float32),
        in_specs=[hbm] * 3,
        out_specs=hbm,
        scratch_shapes=[
            *[pltpu.VMEM(*item) for item in between],
            pltpu.VMEM((rows, cols), jnp.float32),
            *[pltpu.VMEM((width + taps, CHUNK), jnp.bfloat16) for width in plan.part_cols[1:] for _ in range(2)],
            *[pltpu.VMEM((rows, width), jnp.bfloat16) for width in plan.part_cols[1:]],
            pltpu.SemaphoreType.DMA((3,)),
            pltpu.SemaphoreType.DMA((cols // CHUNK,)),
        ],
        name="search",
    )(windows, lhs, plane)


def solution(mesh):
    return jax.shard_map(
        body,
        mesh=mesh,
        in_specs=(P(None, ("beam", "freq")), P(), P()),
        out_specs=P(None, ("beam", "freq")),
        check_vma=False,
    )
```

time: 21.2 us -> 18.2 us (0.86)
  local copies, waits for them, and re-layouts: 2.3 us -> 0 us
  Pallas kernels: 18.7 us -> 18 us
    pallas_call x1, Pallas kernels: 18.7 us -> 7.09 us  [body(): pl.pallas_call(functools.partial(search_kernel, plan), out_shape=jax.Shap...]
    pallas_call x0 -> x1, Pallas kernels: none -> 10.9 us  [body(): pl.pallas_call(functools.partial(gather_kernel, plan), out_shape=tuple((j...]
    unnamed x1 -> x0, local copies, waits for them, and re-layouts: 2.3 us -> none
where the time goes in v4:
time: 18.2 us; the launch traced here: 18 us
  Pallas kernels  18 us (99%)
    pallas_call x1, Pallas kernels, body(): pl.pallas_call(functools.partial(gather_kernel, plan), out_shape=tuple((j...  10.9 us
    pallas_call x1, Pallas kernels, body(): pl.pallas_call(functools.partial(search_kernel, plan), out_shape=jax.Shap...  7.09 us

profile of v4, /device:TPU:1, one launch (start us, length us, event | category | flops | bytes accessed | tf_op | source)
XLA Modules:
  0.0 18.0 jit_solution(1746686635212328312)
XLA Ops:
  0.0 10.9 %gather.1 = (bf16[2,6144]{1,0:T(2,128)(2,1)}, bf16[256,2048]{1,0:T(8,128)(2,1)}, bf16[128,2048]{1,0:T(8,128)(2,1)}) custom-call(bf16[2,2048]{1,0:T(2,128)(2,1)} %spec_ref.1, s32[1,128]{1,0:T(1,128)} %bitcast.1, bf16[2,256,1024]{2,1,0:T(8,128)(2,1)} %bank_ref.1), custom_call_target="tpu_custom_call" | custom-call | tf_op jit(solution)/shard_map/gather/pallas_call | solution.py:319
  10.9 7.1 %search.1 = f32[128,2048]{1,0:T(8,128)} custom-call(bf16[2,6144]{1,0:T(2,128)(2,1)} %get-tuple-element.8.win_ref, bf16[256,2048]{1,0:T(8,128)(2,1)} %get-tuple-element.9.lhs_ref, bf16[128,2048]{1,0:T(8,128)(2,1)} %get-tuple-element.10.plane_ref), custom_call_target="tpu_custom_call" | custom-call | tf_op jit(solution)/shard_map/search/pallas_call | solution.py:340

commit v5 on v4

--- a/solution.py
+++ b/solution.py
@@ -28,6 +28,13 @@
             offset += width + taps if self.offsets[1:] else 0
             slot += (width + taps) // self.granule
         self.width, self.slot_count = offset, slot
+
+    def needs(self, to, source):
+        first = self.held * source
+        found = False
+        for step in self.steps:
+            found = found | ((step * (to + 1) >= first) & (step * to <= first + self.held))
+        return found
 
 
 def sends(plan, me):
@@ -121,12 +128,17 @@
 
     barrier = pltpu.get_barrier_semaphore()
 
-    def greet(step, carry):
+    def greet(step, count):
         peer = lax.rem(me + step, plan.owners)
-        pl.semaphore_signal(barrier, inc=1, device_id={"freq": peer}, device_id_type=pl.DeviceIdType.MESH)
-        return carry
-
-    lax.fori_loop(1, plan.owners, greet, 0)
+        met = plan.needs(me, peer) | plan.needs(peer, me)
+
+        @pl.when(met)
+        def _():
+            pl.semaphore_signal(barrier, inc=1, device_id={"freq": peer}, device_id_type=pl.DeviceIdType.MESH)
+
+        return count + jnp.where(met, 1, 0)
+
+    partners = lax.fori_loop(1, plan.owners, greet, jnp.int32(0))
 
     @pl.when(me == 0)
     def _():
@@ -192,17 +204,6 @@
     fetch_own.wait()
     for task in build(win, shifts, halo, last - halo):
         task()
-    pl.semaphore_wait(barrier, plan.owners - 1)
-    each(lambda copy: copy.start(), lambda copy: copy.start())
-
-    @pl.when(me == 0)
-    def _():
-        for part in range(1, parts):
-            start = plan.offsets[part]
-            pltpu.make_async_copy(
-                win.at[:, 0:size], win_out.at[:, start : start + size], recv_sems.at[plan.slots[part]]
-            ).start()
-
     fetch_index.wait()
     fetch_bank.wait()
     names = lax.broadcasted_iota(jnp.int32, (bank.shape[1], rows), 0)
@@ -220,6 +221,17 @@
         keep(chunk)
     put_lhs = pltpu.make_async_copy(lhs, lhs_out, out_sems.at[0])
     put_lhs.start()
+    pl.semaphore_wait(barrier, partners)
+    each(lambda copy: copy.start(), lambda copy: copy.start())
+
+    @pl.when(me == 0)
+    def _():
+        for part in range(1, parts):
+            start = plan.offsets[part]
+            pltpu.make_async_copy(
+                win.at[:, 0:size], win_out.at[:, start : start + size], recv_sems.at[plan.slots[part]]
+            ).start()
+
     receive(0)
     for task in build(win, shifts, 0, halo) + build(win, shifts, last - halo, last):
         task()

time: 18.2 us -> 18.1 us (level)
  no operation moved by 1% of the time
where the time goes in v5:
time: 18.1 us; the launch traced here: 17.9 us
  Pallas kernels  17.9 us (99%)
    pallas_call x1, Pallas kernels, body(): pl.pallas_call(functools.partial(gather_kernel, plan), out_shape=tuple((j...  10.8 us
    pallas_call x1, Pallas kernels, body(): pl.pallas_call(functools.partial(search_kernel, plan), out_shape=jax.Shap...  7.1 us

profile of v5, /device:TPU:1, one launch (start us, length us, event | category | flops | bytes accessed | tf_op | source)
XLA Modules:
  0.0 17.9 jit_solution(11299818383417365504)
XLA Ops:
  0.0 10.8 %gather.1 = (bf16[2,6144]{1,0:T(2,128)(2,1)}, bf16[256,2048]{1,0:T(8,128)(2,1)}, bf16[128,2048]{1,0:T(8,128)(2,1)}) custom-call(bf16[2,2048]{1,0:T(2,128)(2,1)} %spec_ref.1, s32[1,128]{1,0:T(1,128)} %bitcast.1, bf16[2,256,1024]{2,1,0:T(8,128)(2,1)} %bank_ref.1), custom_call_target="tpu_custom_call" | custom-call | tf_op jit(solution)/shard_map/gather/pallas_call | solution.py:331
  10.8 7.1 %search.1 = f32[128,2048]{1,0:T(8,128)} custom-call(bf16[2,6144]{1,0:T(2,128)(2,1)} %get-tuple-element.8.win_ref, bf16[256,2048]{1,0:T(8,128)(2,1)} %get-tuple-element.9.lhs_ref, bf16[128,2048]{1,0:T(8,128)(2,1)} %get-tuple-element.10.plane_ref), custom_call_target="tpu_custom_call" | custom-call | tf_op jit(solution)/shard_map/search/pallas_call | solution.py:352

commit v6 on v5

--- a/solution.py
+++ b/solution.py
@@ -128,7 +128,8 @@
 
     barrier = pltpu.get_barrier_semaphore()
 
-    def greet(step, count):
+    def greet(step, carry):
+        count, far = carry
         peer = lax.rem(me + step, plan.owners)
         met = plan.needs(me, peer) | plan.needs(peer, me)
 
@@ -136,9 +137,10 @@
         def _():
             pl.semaphore_signal(barrier, inc=1, device_id={"freq": peer}, device_id_type=pl.DeviceIdType.MESH)
 
-        return count + jnp.where(met, 1, 0)
-
-    partners = lax.fori_loop(1, plan.owners, greet, jnp.int32(0))
+        ahead = met & (peer - me >= 7 * plan.owners // 16)
+        return count + jnp.where(met, 1, 0), far + jnp.where(ahead, 1, 0)
+
+    partners, far = lax.fori_loop(1, plan.owners, greet, (jnp.int32(0), jnp.int32(0)))
 
     @pl.when(me == 0)
     def _():
@@ -217,8 +219,12 @@
 
     chunks = plan.cols // CHUNK
     edge = size // CHUNK
-    for chunk in range(edge, chunks - edge):
-        keep(chunk)
+
+    def interior():
+        for chunk in range(edge, chunks - edge):
+            keep(chunk)
+
+    pl.when(far > 0)(interior)
     put_lhs = pltpu.make_async_copy(lhs, lhs_out, out_sems.at[0])
     put_lhs.start()
     pl.semaphore_wait(barrier, partners)
@@ -232,6 +238,7 @@
                 win.at[:, 0:size], win_out.at[:, start : start + size], recv_sems.at[plan.slots[part]]
             ).start()
 
+    pl.when(far == 0)(interior)
     receive(0)
     for task in build(win, shifts, 0, halo) + build(win, shifts, last - halo, last):
         task()

time: 18.1 us -> 18.1 us (level)
  no operation moved by 1% of the time
where the time goes in v6:
time: 18.1 us; the launch traced here: 17.9 us
  Pallas kernels  17.9 us (99%)
    pallas_call x1, Pallas kernels, body(): pl.pallas_call(functools.partial(gather_kernel, plan), out_shape=tuple((j...  10.8 us
    pallas_call x1, Pallas kernels, body(): pl.pallas_call(functools.partial(search_kernel, plan), out_shape=jax.Shap...  7.1 us

profile of v6, /device:TPU:1, one launch (start us, length us, event | category | flops | bytes accessed | tf_op | source)
XLA Modules:
  0.0 17.9 jit_solution(13177626474945335509)
XLA Ops:
  0.0 10.8 %gather.1 = (bf16[2,6144]{1,0:T(2,128)(2,1)}, bf16[256,2048]{1,0:T(8,128)(2,1)}, bf16[128,2048]{1,0:T(8,128)(2,1)}) custom-call(bf16[2,2048]{1,0:T(2,128)(2,1)} %spec_ref.1, s32[1,128]{1,0:T(1,128)} %bitcast.1, bf16[2,256,1024]{2,1,0:T(8,128)(2,1)} %bank_ref.1), custom_call_target="tpu_custom_call" | custom-call | tf_op jit(solution)/shard_map/gather/pallas_call | solution.py:338
  10.8 7.1 %search.1 = f32[128,2048]{1,0:T(8,128)} custom-call(bf16[2,6144]{1,0:T(2,128)(2,1)} %get-tuple-element.8.win_ref, bf16[256,2048]{1,0:T(8,128)(2,1)} %get-tuple-element.9.lhs_ref, bf16[128,2048]{1,0:T(8,128)(2,1)} %get-tuple-element.10.plane_ref), custom_call_target="tpu_custom_call" | custom-call | tf_op jit(solution)/shard_map/search/pallas_call | solution.py:359

commit v7 on v6

--- a/solution.py
+++ b/solution.py
@@ -198,7 +198,7 @@
                 pl.when((spot >= 0) & (spot < plan.held * plan.owners))(land)
 
     def keep(chunk):
-        plane[:, chunk * CHUNK : (chunk + 1) * CHUNK] = power(lhs, shifts, rows, taps, chunk * CHUNK, CHUNK)
+        plane[:, chunk * CHUNK : (chunk + 2) * CHUNK] = power(lhs, shifts, rows, taps, chunk * CHUNK, 2 * CHUNK)
 
     halo = size // LANES
     last = (plan.cols + taps) // LANES - 1
@@ -221,7 +221,7 @@
     edge = size // CHUNK
 
     def interior():
-        for chunk in range(edge, chunks - edge):
+        for chunk in range(edge, chunks - edge, 2):
             keep(chunk)
 
     pl.when(far > 0)(interior)
@@ -242,7 +242,7 @@
     receive(0)
     for task in build(win, shifts, 0, halo) + build(win, shifts, last - halo, last):
         task()
-    for chunk in [*range(edge), *range(chunks - edge, chunks)]:
+    for chunk in [*range(0, edge, 2), *range(chunks - edge, chunks, 2)]:
         keep(chunk)
     put_plane = pltpu.make_async_copy(plane, plane_out, out_sems.at[1])
     put_plane.start()

time: 18.1 us -> 18.1 us (level)
  no operation moved by 1% of the time
where the time goes in v7:
time: 18.1 us; the launch traced here: 17.9 us
  Pallas kernels  17.9 us (99%)
    pallas_call x1, Pallas kernels, body(): pl.pallas_call(functools.partial(gather_kernel, plan), out_shape=tuple((j...  10.8 us
    pallas_call x1, Pallas kernels, body(): pl.pallas_call(functools.partial(search_kernel, plan), out_shape=jax.Shap...  7.1 us

profile of v7, /device:TPU:1, one launch (start us, length us, event | category | flops | bytes accessed | tf_op | source)
XLA Modules:
  0.0 17.9 jit_solution(10266624349594798800)
XLA Ops:
  0.0 10.8 %gather.1 = (bf16[2,6144]{1,0:T(2,128)(2,1)}, bf16[256,2048]{1,0:T(8,128)(2,1)}, bf16[128,2048]{1,0:T(8,128)(2,1)}) custom-call(bf16[2,2048]{1,0:T(2,128)(2,1)} %spec_ref.1, s32[1,128]{1,0:T(1,128)} %bitcast.1, bf16[2,256,1024]{2,1,0:T(8,128)(2,1)} %bank_ref.1), custom_call_target="tpu_custom_call" | custom-call | tf_op jit(solution)/shard_map/gather/pallas_call | solution.py:338
  10.8 7.1 %search.1 = f32[128,2048]{1,0:T(8,128)} custom-call(bf16[2,6144]{1,0:T(2,128)(2,1)} %get-tuple-element.8.win_ref, bf16[256,2048]{1,0:T(8,128)(2,1)} %get-tuple-element.9.lhs_ref, bf16[128,2048]{1,0:T(8,128)(2,1)} %get-tuple-element.10.plane_ref), custom_call_target="tpu_custom_call" | custom-call | tf_op jit(solution)/shard_map/search/pallas_call | solution.py:359
